TPU v7x, 512 devices: a whole 4x4x16 slice. The times are simulated.
512 devices in a mesh: row: 32 (over z, x_lo), col: 16 (over x_hi, y, core).
Axes of the slice: x: 4 (x_hi: 2, x_lo: 2; x = x_hi * 2 + x_lo), y: 4, z: 16, core: 2. Of those that a mesh axis runs over, the one named last changes fastest.
Arguments:
- matrix: bfloat16 [8192, 24576], P('row', 'col'), may hold values from -6 to 6
- pivots: int32 [2, 256], replicated, may hold values from 256 to 8191, as said below
- lower_inverse: bfloat16 [2, 256, 256], replicated, as said below
- upper_inverse: bfloat16 [2, 256, 256], replicated, as said below
Outputs:
- factored: bfloat16 [8192, 24576], P('row', 'col')
Inputs may be any that keep to these rules, and one draw needn't show every extreme that they name: Matrix row numbers (not stored rows). Within pivots[s] the entries are distinct and lie in (s + 1) * 256 .. 8191; each step lists (s + 1) * 256 and 8191. Each lower_inverse[s] has ones on the diagonal and zeros above it. Each upper_inverse[s] is zero below the diagonal.
All inputs are finite; a program needn't handle non-finite values.
Results may differ from a plain program's by a relative error of at most 0.0083.
Values may be sent and summed in bfloat16 or wider, within the bound.
A program may use at most 64 MiB of HBM per device.

v0:
```python
import jax
import jax.numpy as jnp
from jax import lax
from jax.sharding import PartitionSpec as P


def spread(value, axis, source):
    kept = jnp.where(lax.axis_index(axis) == source, value, 0).astype(value.dtype)
    return lax.psum(kept, axis)


def body(matrix, pivots, lower_inverse, upper_inverse):
    local_rows, local_cols = matrix.shape
    block = lower_inverse.shape[1]
    grid_rows = lax.axis_size("row")
    grid_cols = lax.axis_size("col")
    my_row = lax.axis_index("row")
    my_col = lax.axis_index("col")
    row_ids = jnp.arange(local_rows, dtype=jnp.int32)
    row_global = row_ids // block * grid_rows + my_row
    col_global = jnp.arange(local_cols, dtype=jnp.int32) // block * grid_cols + my_col
    current = matrix
    for step_index in range(2):
        top_owner = step_index % grid_rows
        top_start = step_index // grid_rows * block
        panel_owner = step_index % grid_cols
        panel_start = step_index // grid_cols * block
        chosen = pivots[step_index]
        owner_rows = chosen // block % grid_rows
        local_index = chosen // (block * grid_rows) * block + chosen % block
        owned = owner_rows == my_row
        match = jnp.logical_and(row_ids[:, None] == local_index[None, :], owned[None, :])
        selector = match.astype(jnp.bfloat16)
        candidates = lax.dot_general(
            selector, current, (((0,), (0,)), ((), ())), preferred_element_type=jnp.float32
        )
        top_here = current
        is_top = my_row == top_owner
        new_top = lax.psum(candidates.astype(jnp.bfloat16), "row")
        displaced_rows = spread(top_here, "row", top_owner)
        placed = jnp.dot(selector, displaced_rows, preferred_element_type=jnp.float32).astype(
            jnp.bfloat16
        )
        hit = jnp.any(match, axis=1)
        current = jnp.where(hit[:, None], placed, current)
        current = current.at[top_start : top_start + block].set(jnp.where(is_top, new_top, current))
        row_live = row_global > step_index
        col_live = col_global > step_index
        panel = current[:, panel_start : panel_start + block]
        lower_part = jnp.dot(
            panel, upper_inverse[step_index], preferred_element_type=jnp.float32
        ).astype(jnp.bfloat16)
        lower_part = jnp.where(row_live[:, None], lower_part, jnp.zeros_like(lower_part))
        lower_all = spread(lower_part, "col", panel_owner)
        top_rows_now = current
        upper_mine = jnp.dot(
            lower_inverse[step_index], top_rows_now, preferred_element_type=jnp.float32
        ).astype(jnp.bfloat16)
        upper_mine = jnp.where(col_live[None, :], upper_mine, jnp.zeros_like(upper_mine))
        upper_part = spread(upper_mine, "row", top_owner)
        product = jnp.dot(lower_all, upper_part, preferred_element_type=jnp.float32)
        updated = (current.astype(jnp.float32) - product).astype(jnp.bfloat16)
        panel_old = updated[:, panel_start : panel_start + block]
        keep_lower = jnp.logical_and(my_col == panel_owner, row_live[:, None])
        updated = updated.at[:, panel_start : panel_start + block].set(
            jnp.where(keep_lower, lower_all, panel_old)
        )
        top_old = updated
        keep_upper = jnp.logical_and(is_top, col_live[None, :])
        updated = updated.at[top_start : top_start + block].set(
            jnp.where(keep_upper, upper_part, top_old)
        )
        current = updated
    return current


def solution(mesh):
    placed = (P("row", "col"), P(), P(), P())
    return jax.shard_map(
        body, mesh=mesh, in_specs=placed, out_specs=P("row", "col"), check_vma=False
    )
```

profile of v0, /device:TPU:24, one launch (start us, length us, event | category | flops | bytes accessed | tf_op | source)
XLA Modules:
  0.0 1410.0 jit_solution(4308838548995504548)
XLA Ops:
  6.5 0.8 fusion.51
  7.3 0.8 compare_reduce_fusion.1
  8.1 2.2 broadcast_select_fusion
  10.3 1.3 convolution_convert_fusion.5
  11.6 0.0 all-reduce.11.cloned.1.call-start
  11.7 0.1 fusion.22
  11.8 272.3 %all-reduce.19.cloned.1.call-done = (bf16[256,1536]{1,0:T(8,128)(2,1)}, bf16[256,1536]{1,0:T(8,128)(2,1)}) async-done(((bf16[256,1536]{1,0:T(8,128)(2,1)}, bf16[256,1536]{1,0:T(8,128)(2,1)}), (bf16[256,1536]{1,0:T(8,128)(2,1)}, bf16[256,1536]{1,0:T(8,128)(2,1)})) %all-reduce.19.cloned.1.call-update) | async-done | bytes 1572880 | tf_op jit(solution)/shard_map/psum | solution.py:39
  284.1 1.8 fusion.3
  285.9 0.9 fusion.13
  286.8 0.0 all-reduce.11.cloned.1.call-update
  286.8 0.0 all-reduce.9.cloned.1.call-start
  286.9 1.3 fusion.11
  288.1 0.0 all-reduce.17.cloned.1.call-start
  288.2 0.6 compare_reduce_fusion.2
  288.9 146.1 %all-reduce.11.cloned.1.call-done = bf16[256,256]{1,0:T(8,128)(2,1)} async-done(((bf16[256,256]{1,0:T(8,128)(2,1)}), bf16[256,256]{1,0:T(8,128)(2,1)}) %all-reduce.11.cloned.1.call-update) | async-done | bytes 131088 | tf_op jit(solution)/shard_map/psum | solution.py:9
  434.9 271.1 %all-reduce.9.cloned.1.call-done = bf16[256,1536]{1,0:T(8,128)(2,1)} async-done(((bf16[256,1536]{1,0:T(8,128)(2,1)}), bf16[256,1536]{1,0:T(8,128)(2,1)}) %all-reduce.9.cloned.1.call-update) | async-done | bytes 786448 | tf_op jit(solution)/shard_map/psum | solution.py:9
  706.0 1.6 fusion
  707.6 0.7 fusion.24
  708.3 1.0 broadcast_select_fusion.2
  709.3 1.3 convolution_convert_fusion.3
  710.7 0.0 all-reduce.15.cloned.1.call-start
  710.7 0.1 fusion.18
  710.9 267.4 %all-reduce.17.cloned.1.call-done = (bf16[256,1536]{1,0:T(8,128)(2,1)}, bf16[256,1536]{1,0:T(8,128)(2,1)}) async-done(((bf16[256,1536]{1,0:T(8,128)(2,1)}, bf16[256,1536]{1,0:T(8,128)(2,1)}), (bf16[256,1536]{1,0:T(8,128)(2,1)}, bf16[256,1536]{1,0:T(8,128)(2,1)})) %all-reduce.17.cloned.1.call-update) | async-done | bytes 1572880 | tf_op jit(solution)/shard_map/psum | solution.py:39
  978.3 1.5 fusion.5
  979.8 0.9 fusion.15
  980.7 0.0 all-reduce.13.cloned.1.call-start
  980.7 1.3 fusion.10
  982.0 146.7 %all-reduce.15.cloned.1.call-done = bf16[256,256]{1,0:T(8,128)(2,1)} async-done(((bf16[256,256]{1,0:T(8,128)(2,1)}), bf16[256,256]{1,0:T(8,128)(2,1)}) %all-reduce.15.cloned.1.call-update) | async-done | bytes 131088 | tf_op jit(solution)/shard_map/psum | solution.py:9
  1128.7 271.2 %all-reduce.13.cloned.1.call-done = bf16[256,1536]{1,0:T(8,128)(2,1)} async-done(((bf16[256,1536]{1,0:T(8,128)(2,1)}), bf16[256,1536]{1,0:T(8,128)(2,1)}) %all-reduce.13.cloned.1.call-update) | async-done | bytes 786448 | tf_op jit(solution)/shard_map/psum | solution.py:9
  1399.9 1.6 fusion.1
  1401.5 0.7 fusion.25
  1402.2 1.0 broadcast_select_fusion.3
  (28 shorter events, 0.2 us)
Async XLA Ops:
  6.5 277.6 %all-reduce.19.cloned.1.call-start = ((), (), s32[]{:S(2)}) async-start(), calls=%async_computation.5 | async-start | bytes 3145728 | tf_op jit(solution)/shard_map/psum | solution.py:39
  8.1 2.2 copy-start
  11.6 423.3 %all-reduce.11.cloned.1.call-start = ((), (), s32[]{:S(2)}) async-start(), calls=%async_computation.1 | async-start | bytes 262144 | tf_op jit(solution)/shard_map/psum | solution.py:9
  284.1 1.8 copy-start.5
  284.1 2.8 copy-start.6
  286.8 419.2 %all-reduce.9.cloned.1.call-start = ((), (), s32[]{:S(2)}) async-start(), calls=%async_computation | async-start | bytes 1572864 | tf_op jit(solution)/shard_map/psum | solution.py:9
  288.1 690.1 %all-reduce.17.cloned.1.call-start = ((), (), s32[]{:S(2)}) async-start(), calls=%async_computation.4 | async-start | bytes 3145728 | tf_op jit(solution)/shard_map/psum | solution.py:39
  434.9 272.7 %copy-start.3 = (bf16[256,256]{1,0:T(8,128)(2,1)S(1)}, bf16[256,256]{1,0:T(8,128)(2,1)}, u32[]{:S(2)}) copy-start(bf16[256,256]{1,0:T(8,128)(2,1)} %all-reduce.11.cloned.1.call-done) | copy-start | bytes 393220
  706.0 2.3 copy-start.1
  710.7 418.0 %all-reduce.15.cloned.1.call-start = ((), (), s32[]{:S(2)}) async-start(), calls=%async_computation.3 | async-start | bytes 262144 | tf_op jit(solution)/shard_map/psum | solution.py:9
  980.7 419.2 %all-reduce.13.cloned.1.call-start = ((), (), s32[]{:S(2)}) async-start(), calls=%async_computation.2 | async-start | bytes 1572864 | tf_op jit(solution)/shard_map/psum | solution.py:9
  1128.7 272.8 %copy-start.4 = (bf16[256,256]{1,0:T(8,128)(2,1)S(1)}, bf16[256,256]{1,0:T(8,128)(2,1)}, u32[]{:S(2)}) copy-start(bf16[256,256]{1,0:T(8,128)(2,1)} %all-reduce.15.cloned.1.call-done) | copy-start | bytes 393220
  1399.9 2.3 copy-start.2
Sparse Core Ops, SparseCore 0:
  11.7 272.3 all-reduce.18
  287.2 147.6 all-reduce.10
  437.8 268.1 all-reduce.8
  710.8 267.4 all-reduce.16
  981.0 147.6 all-reduce.14
  1131.7 268.1 all-reduce.12
where the time goes:
time: 1410 us
  waiting for transfers between devices  1370 us (97%)
    psum x4, waiting for transfers between devices, spread(): return lax.psum(kept, axis)  835 us
    psum x2, waiting for transfers between devices, body(): new_top = lax.psum(candidates.astype(jnp.bfloat16), 'row')  540 us
  transfers between devices with their start and end apart: 6, of which 6 were waited for; matrix products, arithmetic and copies ran while one was open for 0% of the time, Pallas kernels for 0%

commit v1 on v0

v1 whole, which is shorter than its diff:
```python
import functools

import jax
import jax.numpy as jnp
from jax import lax
from jax.experimental import pallas as pl
from jax.experimental.pallas import tpu as pltpu
from jax.sharding import PartitionSpec as P

MESH = pl.DeviceIdType.MESH
F32 = jnp.float32
BF16 = jnp.bfloat16
SUB = 3


def dot(a, b):
    return jnp.dot(a, b, preferred_element_type=F32)


def kernel(
    rows_n, cols_n,
    a_ref, piv_ref, lo_ref, up_ref, o_ref,
    cand, rp, rm, fin, xb, tb, te, db, de, pb, gsel, own_ref,
    rp_s, rp_r, rm_s, rm_r, x_s, x_r, e_s, e_r,
    tp_s, tp_r, tx_s, tx_r, dp_s, dp_r, dx_s, dx_r,
    pan_s, pan_r, sc_s, sc_r,
):
    block = lo_ref.shape[1]
    zn = rows_n // 2
    half = zn // 2
    width = cand.shape[-1]
    per = block // zn
    row = lax.axis_index("row")
    col = lax.axis_index("col")
    z = row // 2
    xl = lax.rem(row, 2)
    up_id = (lax.rem(row + 2, rows_n), col)
    down_id = (lax.rem(row + rows_n - 2, rows_n), col)
    pair_id = (row + 1 - 2 * xl, col)
    is_root = z == 0
    home = lambda k: lax.rem(k + 4 * zn, zn)

    barrier = pltpu.get_barrier_semaphore()
    for dest in (up_id, down_id, pair_id):
        pl.semaphore_signal(barrier, inc=1, device_id=dest, device_id_type=MESH)
    for p in range(2):
        @pl.when(col != p)
        def _():
            pl.semaphore_signal(barrier, inc=1, device_id=(row, p), device_id_type=MESH)

    @pl.when(z != 0)
    def _():
        pl.semaphore_signal(barrier, inc=1, device_id=(xl, col), device_id_type=MESH)

    base = (row * block).astype(F32)
    ii = lax.broadcasted_iota(jnp.int32, (block, block), 0).astype(F32)
    jj = lax.broadcasted_iota(jnp.int32, (block, block), 1).astype(F32)
    p0r = piv_ref[0:1, :].astype(F32)
    p1r = piv_ref[1:2, :].astype(F32)
    eye = ii == jj
    p0c = jnp.sum(jnp.where(eye, p0r, 0.0), axis=1, keepdims=True)
    p1c = jnp.sum(jnp.where(eye, p1r, 0.0), axis=1, keepdims=True)
    q1c = p1c + jnp.sum(jnp.where(p1c == p0r, jj - p1c, 0.0), axis=1, keepdims=True)
    sel0 = jnp.where(p0c == base + jj, 1.0, 0.0).astype(BF16)
    sel1 = jnp.where(q1c == base + jj, 1.0, 0.0).astype(BF16)
    for s in range(SUB):
        a_s = a_ref[:, s * width : (s + 1) * width]
        cand[s, :, 0] = dot(sel0, a_s).astype(BF16).reshape(zn, per, width)
        cand[s, :, 1] = dot(sel1, a_s).astype(BF16).reshape(zn, per, width)

    h0 = jnp.where(base + ii == p0r, 1.0, 0.0)
    h1 = jnp.where(base + ii == p1r, 1.0, 0.0)
    any0 = jnp.sum(h0, axis=1, keepdims=True)
    any1 = jnp.sum(h1, axis=1, keepdims=True)
    into1 = jnp.where(p0r == block + ii, 1.0, 0.0)
    from0 = jnp.sum(jnp.where(p0c == block + jj, 1.0, 0.0), axis=0, keepdims=True)
    via = dot(h1.astype(BF16), into1.astype(BF16))
    gsel[:, 0:block] = (via + h0 * (1.0 - any1)).astype(BF16)
    gsel[:, block : 2 * block] = (h1 * (1.0 - from0)).astype(BF16)
    own_ref[...] = jnp.broadcast_to((1.0 - any1) * (1.0 - any0), own_ref.shape)

    waits = 3 + jnp.where(col < 2, cols_n - 1, 0) + jnp.where(is_root, zn - 1, 0)
    pl.semaphore_wait(barrier, waits)

    def remote(src, dst, ssem, rsem, dest):
        return pltpu.make_async_remote_copy(
            src_ref=src, dst_ref=dst, send_sem=ssem, recv_sem=rsem,
            device_id=dest, device_id_type=MESH,
        )

    def panel_copy(p, other):
        return remote(
            a_ref.at[:, pl.ds(0, block)], pb.at[:, pl.ds(p * block, block)],
            pan_s.at[other], pan_r.at[p], (row, other),
        )

    def panel(p, action):
        @pl.when(col == p)
        def _():
            for other in range(cols_n):
                if other != p:
                    action(panel_copy(p, other))

    for p in range(2):
        panel(p, lambda c: c.start())

        @pl.when(col == p)
        def _():
            pb[:, p * block : (p + 1) * block] = a_ref[:, 0:block]

    def scatter_main(k):
        return remote(
            a_ref.at[pl.ds(k * per, per)], db.at[xl, k], sc_s.at[0, k], sc_r.at[0],
            (2 * k + xl, col),
        )

    def scatter_ext(k):
        return remote(
            pb.at[pl.ds(k * per, per)], de.at[xl, k], sc_s.at[1, k], sc_r.at[1],
            (2 * k + xl, col),
        )

    def plus(t, s):
        src = cand.at[s, home(z + half)] if t == 0 else rp.at[t - 1, s]
        return remote(src, rp.at[t, s], rp_s.at[t, s], rp_r.at[t, s], up_id)

    def minus(t, s):
        src = cand.at[s, home(z - half + 1)] if t == 0 else rm.at[t - 1, s]
        return remote(src, rm.at[t, s], rm_s.at[t, s], rm_r.at[t, s], down_id)

    for s in range(SUB):
        plus(0, s).start()
        minus(0, s).start()

    @pl.when(is_root)
    def _():
        for k in range(1, zn):
            scatter_main(k).start()
        db[xl, 0] = a_ref[0:per, :]

    for t in range(1, half):
        for s in range(SUB):
            plus(t - 1, s).wait_recv()
            rp[t - 1, s] = rp[t - 1, s] + cand[s, home(z + half - t)]
            plus(t, s).start()
            if t < half - 1:
                minus(t - 1, s).wait_recv()
                rm[t - 1, s] = rm[t - 1, s] + cand[s, home(z - half + 1 + t)]
                minus(t, s).start()
        if t == half // 2:
            for p in range(2):
                @pl.when(col != p)
                def _():
                    panel_copy(p, 0).wait_recv()

            @pl.when(is_root)
            def _():
                for k in range(1, zn):
                    scatter_ext(k).start()
                de[xl, 0] = pb[0:per, :]

    def swap(s):
        return remote(fin.at[s, 1 - xl], xb.at[s], x_s.at[s], x_r.at[s], pair_id)

    for s in range(SUB):
        plus(half - 1, s).wait_recv()
        minus(half - 2, s).wait_recv()
        fin[s] = cand[s, z] + rp[half - 1, s] + rm[half - 2, s]
        swap(s).start()
    for s in range(SUB):
        swap(s).wait_recv()
        tb[xl, s, z] = fin[s, xl] + xb[s]

    source = 1 - xl

    def ext_copy(other):
        return remote(
            tb.at[xl, 0, z, :, pl.ds(0, block)], te.at[xl, z], e_s.at[other], e_r, (row, other)
        )

    for p in range(2):
        @pl.when(jnp.logical_and(col == p, source == p))
        def _():
            for other in range(cols_n):
                if other != p:
                    ext_copy(other).start()
            te[xl, z] = tb[xl, 0, z, :, 0:block]

    @pl.when(z != 0)
    def _():
        scatter_main(1).wait_recv()
        scatter_ext(1).wait_recv()

    n_t, n_d = SUB + 1, 2

    def t_piece(part, j, k):
        return tb.at[part, j, k] if j < SUB else te.at[part, k]

    def d_piece(part, j, k):
        return db.at[part, k] if j == 0 else de.at[part, k]

    def along(piece, ssem, rsem, d, t, j):
        k = home(z - t) if d == 0 else home(z + t)
        ref = piece(xl, j, k)
        slot = t if d == 0 else half + t
        return remote(ref, ref, ssem.at[slot, j], rsem.at[slot, j], up_id if d == 0 else down_id)

    def across(piece, ssem, rsem, d, t, j):
        k = home(z - t) if d == 0 else home(z + t)
        ref = piece(xl, j, k)
        slot = t if d == 0 else half + t
        return remote(ref, ref, ssem.at[slot, j], rsem.at[slot, j], pair_id)

    streams = ((t_piece, n_t, tp_s, tp_r, tx_s, tx_r), (d_piece, n_d, dp_s, dp_r, dx_s, dx_r))

    def not_source(action):
        @pl.when(col != source)
        def _():
            action()

    for t in range(half + 1):
        for piece, n, ps, pr, xs, xr in streams:
            for j in range(n):
                if t == 0:
                    if piece is t_piece and j == SUB:
                        not_source(lambda: ext_copy(0).wait_recv())
                    for d in range(2):
                        along(piece, ps, pr, d, 0, j).start()
                    across(piece, xs, xr, 0, 0, j).start()
                else:
                    for d in range(2):
                        if d == 0 or t < half:
                            along(piece, ps, pr, d, t - 1, j).wait_recv()
                            if t < (half if d == 0 else half - 1):
                                along(piece, ps, pr, d, t, j).start()
                            across(piece, xs, xr, d, t, j).start()
    for piece, n, ps, pr, xs, xr in streams:
        for j in range(n):
            for t in range(half + 1):
                across(piece, xs, xr, 0, t, j).wait_recv()
                if 0 < t < half:
                    across(piece, xs, xr, 1, t, j).wait_recv()

    lo0, lo1, up0, up1 = lo_ref[0], lo_ref[1], up_ref[0], up_ref[1]
    ext0 = te[0].reshape(block, block)
    ext1 = te[1].reshape(block, block)
    lower_t = dot(ext1, up0).astype(BF16)

    def top(s):
        t0 = tb[0, s].reshape(block, width)
        t1 = tb[1, s].reshape(block, width)
        u0 = dot(lo0, t0).astype(BF16)
        return t0, t1, u0

    def second(t1, u0):
        t1u = (t1.astype(F32) - dot(lower_t, u0)).astype(BF16)
        return t1u, dot(lo1, t1u).astype(BF16)

    def cols(s):
        return slice(s * width, (s + 1) * width)

    @pl.when(row == 0)
    def _():
        for s in range(SUB):
            t0, _, u0 = top(s)
            o_ref[:, cols(s)] = u0

        @pl.when(col == 0)
        def _():
            o_ref[:, 0:block] = tb[0, 0].reshape(block, width)[:, 0:block]

    @pl.when(row == 1)
    def _():
        for s in range(SUB):
            _, t1, u0 = top(s)
            t1u, u1 = second(t1, u0)
            o_ref[:, cols(s)] = u1
            if s == 0:
                @pl.when(col == 1)
                def _():
                    o_ref[:, 0:block] = t1u[:, 0:block]

        @pl.when(col == 0)
        def _():
            o_ref[:, 0:block] = lower_t

    @pl.when(row > 1)
    def _():
        own = own_ref[:, 0:1]
        g = gsel[...]
        moved = jnp.concatenate([de[0].reshape(block, 2 * block), de[1].reshape(block, 2 * block)], axis=0)
        pan = dot(g, moved) + own * pb[...].astype(F32)
        l0 = dot(pan[:, 0:block].astype(BF16), up0).astype(BF16)
        u0e = dot(lo0, ext0).astype(BF16)
        y1 = (pan[:, block : 2 * block] - dot(l0, u0e)).astype(BF16)
        l1 = dot(y1, up1).astype(BF16)
        ll = jnp.concatenate([l0, l1], axis=1)
        for s in range(SUB):
            _, t1, u0 = top(s)
            _, u1 = second(t1, u0)
            d0 = db[0, :, :, cols(s)].reshape(block, width)
            d1 = db[1, :, :, cols(s)].reshape(block, width)
            x = dot(g, jnp.concatenate([d0, d1], axis=0)) + own * a_ref[:, cols(s)].astype(F32)
            uu = jnp.concatenate([u0, u1], axis=0)
            o_ref[:, cols(s)] = (x - dot(ll, uu)).astype(BF16)

        @pl.when(col == 0)
        def _():
            o_ref[:, 0:block] = l0

        @pl.when(col == 1)
        def _():
            o_ref[:, 0:block] = l1

    for p in range(2):
        panel(p, lambda c: c.wait_send())

    @pl.when(is_root)
    def _():
        for k in range(1, zn):
            scatter_main(k).wait_send()
            scatter_ext(k).wait_send()

    for s in range(SUB):
        for t in range(half):
            plus(t, s).wait_send()
            if t < half - 1:
                minus(t, s).wait_send()
        swap(s).wait_send()
    for p in range(2):
        @pl.when(jnp.logical_and(col == p, source == p))
        def _():
            for other in range(cols_n):
                if other != p:
                    ext_copy(other).wait_send()

    for piece, n, ps, pr, xs, xr in streams:
        for j in range(n):
            for t in range(half + 1):
                across(piece, xs, xr, 0, t, j).wait_send()
                if 0 < t < half:
                    across(piece, xs, xr, 1, t, j).wait_send()
                if t < half:
                    along(piece, ps, pr, 0, t, j).wait_send()
                if t < half - 1:
                    along(piece, ps, pr, 1, t, j).wait_send()


def body(matrix, pivots, lower_inverse, upper_inverse):
    local_rows, local_cols = matrix.shape
    block = lower_inverse.shape[1]
    rows_n = lax.axis_size("row")
    cols_n = lax.axis_size("col")
    zn = rows_n // 2
    half = zn // 2
    per = block // zn
    width = local_cols // SUB
    sem = pltpu.SemaphoreType.DMA
    vmem = pltpu.VMEM
    return pl.pallas_call(
        functools.partial(kernel, rows_n, cols_n),
        out_shape=jax.ShapeDtypeStruct((local_rows, local_cols), BF16),
        in_specs=[pl.BlockSpec(memory_space=pltpu.VMEM)] * 4,
        out_specs=pl.BlockSpec(memory_space=pltpu.VMEM),
        scratch_shapes=[
            vmem((SUB, zn, 2, per, width), BF16),
            vmem((half, SUB, 2, per, width), BF16),
            vmem((half - 1, SUB, 2, per, width), BF16),
            vmem((SUB, 2, per, width), BF16),
            vmem((SUB, per, width), BF16),
            vmem((2, SUB, zn, per, width), BF16),
            vmem((2, zn, per, block), BF16),
            vmem((2, zn, per, local_cols), BF16),
            vmem((2, zn, per, 2 * block), BF16),
            vmem((block, 2 * block), BF16),
            vmem((block, 2 * block), BF16),
            vmem((block, 128), F32),
            sem((half, SUB)), sem((half, SUB)),
            sem((half - 1, SUB)), sem((half - 1, SUB)),
            sem((SUB,)), sem((SUB,)),
            sem((cols_n,)), sem(()),
            sem((2 * half - 1, SUB + 1)), sem((2 * half - 1, SUB + 1)),
            sem((2 * half, SUB + 1)), sem((2 * half, SUB + 1)),
            sem((2 * half - 1, 2)), sem((2 * half - 1, 2)),
            sem((2 * half, 2)), sem((2 * half, 2)),
            sem((cols_n,)), sem((2,)),
            sem((2, zn)), sem((2,)),
        ],
        compiler_params=pltpu.CompilerParams(
            collective_id=0, has_side_effects=True, vmem_limit_bytes=56 << 20
        ),
    )(matrix, pivots, lower_inverse, upper_inverse)


def solution(mesh):
    placed = (P("row", "col"), P(), P(), P())
    return jax.shard_map(
        body, mesh=mesh, in_specs=placed, out_specs=P("row", "col"), check_vma=False
    )
```

time: 1410 us -> 111 us (0.08)
  the two profiles are of different devices: /device:TPU:24 before, /device:TPU:60 now
where the time goes in v1:
time: 111 us; the launch traced here: 110 us
  Pallas kernels  108 us (97%)
  local copies, waits for them, and re-layouts  2.06 us (2%)
    pallas_call x1, Pallas kernels, body(): pl.pallas_call(functools.partial(kernel, rows_n, cols_n), out_shape=jax.S...  108 us

profile of v1, /device:TPU:60, one launch (start us, length us, event | category | flops | bytes accessed | tf_op | source)
XLA Modules:
  0.0 110.4 jit_solution(15578409662743782749)
XLA Ops:
  0.0 108.3 %shard_map.46 = bf16[256,1536]{1,0:T(8,128)(2,1)} custom-call(bf16[256,1536]{1,0:T(8,128)(2,1)} %a_ref.1, s32[2,256]{1,0:T(2,128)} %piv_ref.1, bf16[2,256,256]{2,1,0:T(8,128)(2,1)} %lo_ref.1, bf16[2,256,256]{2,1,0:T(8,128)(2,1)} %up_ref.1), custom_call_target="tpu_custom_call" | custom-call | tf_op jit(solution)/shard_map/pallas_call | solution.py:360
  108.3 2.1 %copy.6 = bf16[256,1536]{1,0:T(8,128)(2,1)} copy(bf16[256,1536]{1,0:T(8,128)(2,1)} %shard_map.46) | data formatting | bytes 1572864

commit v2 on v0

v2 whole, which is shorter than its diff:
```python
import functools

import jax
import jax.numpy as jnp
from jax import lax
from jax.experimental import pallas as pl
from jax.experimental.pallas import tpu as pltpu
from jax.sharding import PartitionSpec as P

MESH = pl.DeviceIdType.MESH
F32 = jnp.float32
BF16 = jnp.bfloat16
SUB = 3
T_HOP = 2
D_HOP = 2
FULL = 0
D_START = 2
PAN_A = 0
PAN_X = 2
PAN_B = 3
DO_D = True
DO_COMP = True
DO_T = True
DO_PAN = True
D_CROSS = True
SC_N = 15
SC_0 = 0


def dot(a, b):
    return jnp.dot(a, b, preferred_element_type=F32)


def kernel(
    rows_n, cols_n,
    a_ref, piv_ref, lo_ref, up_ref, o_ref,
    cand, lead, selh, rp, rm, fin, xb, tb, te, db, pb, gsel, own_ref,
    rp_s, rp_r, rm_s, rm_r, x_s, x_r, e_s, e_r,
    tp_s, tp_r, tx_s, tx_r, dp_s, dp_r, dx_s, dx_r,
    pan_s, pan_r, sc_s, sc_r,
):
    block = lo_ref.shape[1]
    zn = rows_n // 2
    half = zn // 2
    width = cand.shape[-1]
    per = block // zn
    row = lax.axis_index("row")
    col = lax.axis_index("col")
    z = row // 2
    xl = lax.rem(row, 2)
    core = lax.rem(col, 2)
    pair_id = (row + 1 - 2 * xl, col)
    core_id = (row, col + 1 - 2 * core)
    is_root = z == 0
    source = 1 - xl

    def home(k):
        return lax.rem(k + 4 * zn, zn)

    def at_z(i):
        return (2 * home(z + i) + xl, col)

    barrier = pltpu.get_barrier_semaphore()

    def greet(dest):
        pl.semaphore_signal(barrier, inc=1, device_id=dest, device_id_type=MESH)

    reach = max(T_HOP, D_HOP)
    for i in range(1, reach + 1):
        greet(at_z(i))
        greet(at_z(-i))
    greet(pair_id)
    greet(core_id)
    for p in range(2):
        @pl.when(col != p)
        def _():
            greet((row, p))

    @pl.when(col > cols_n // 2 + 1)
    def _():
        greet((row, cols_n // 2 + core))

    @pl.when(z != 0)
    def _():
        greet((xl, col))

    base = (row * block).astype(F32)
    ii = lax.broadcasted_iota(jnp.int32, (block, block), 0).astype(F32)
    jj = lax.broadcasted_iota(jnp.int32, (block, block), 1).astype(F32)
    p0r = piv_ref[0:1, :].astype(F32)
    p1r = piv_ref[1:2, :].astype(F32)
    eye = ii == jj
    p0c = jnp.sum(jnp.where(eye, p0r, 0.0), axis=1, keepdims=True)
    p1c = jnp.sum(jnp.where(eye, p1r, 0.0), axis=1, keepdims=True)
    q1c = p1c + jnp.sum(jnp.where(p1c == p0r, jj - p1c, 0.0), axis=1, keepdims=True)
    selh[:, 0] = jnp.where(p0c == base + jj, 1.0, 0.0).astype(BF16).reshape(zn, per, block)
    selh[:, 1] = jnp.where(q1c == base + jj, 1.0, 0.0).astype(BF16).reshape(zn, per, block)
    firsts = (home(z + half), home(z - half + 1))
    for d in range(2):
        sel = selh[firsts[d]].reshape(2 * per, block)
        for s in range(SUB):
            part = dot(sel, a_ref[:, s * width : (s + 1) * width]).astype(BF16)
            lead[d, s] = part.reshape(2, per, width)

    waits = 2 * reach + 2 + jnp.where(col < 2, cols_n - 1, 0) + jnp.where(col // 2 == cols_n // 4, cols_n // 4 - 1, 0) + jnp.where(is_root, zn - 1, 0)
    pl.semaphore_wait(barrier, waits)

    def remote(src, dst, ssem, rsem, dest):
        return pltpu.make_async_remote_copy(
            src_ref=src, dst_ref=dst, send_sem=ssem, recv_sem=rsem,
            device_id=dest, device_id_type=MESH,
        )

    def plus(t, s):
        src = lead.at[0, s] if t == 0 else rp.at[t - 1, s]
        return remote(src, rp.at[t, s], rp_s.at[t, s], rp_r.at[t, s], at_z(1))

    def minus(t, s):
        src = lead.at[1, s] if t == 0 else rm.at[t - 1, s]
        return remote(src, rm.at[t, s], rm_s.at[t, s], rm_r.at[t, s], at_z(-1))

    def reduce_step(t):
        for s in range(SUB):
            if t == 0:
                plus(0, s).start()
                minus(0, s).start()
                continue
            plus(t - 1, s).wait_recv()
            rp[t - 1, s] = rp[t - 1, s] + cand[s, home(z + half - t)]
            plus(t, s).start()
            if t < half - 1:
                minus(t - 1, s).wait_recv()
                rm[t - 1, s] = rm[t - 1, s] + cand[s, home(z - half + 1 + t)]
                minus(t, s).start()

    def candidates():
        for s in range(SUB):
            sel = selh[...].reshape(zn * 2 * per, block)
            part = dot(sel, a_ref[:, s * width : (s + 1) * width]).astype(BF16)
            cand[s] = part.reshape(zn, 2, per, width)

    def sources():
        h0 = jnp.where(base + ii == p0r, 1.0, 0.0)
        h1 = jnp.where(base + ii == p1r, 1.0, 0.0)
        any0 = jnp.sum(h0, axis=1, keepdims=True)
        any1 = jnp.sum(h1, axis=1, keepdims=True)
        into1 = jnp.where(p0r == block + ii, 1.0, 0.0)
        from0 = jnp.sum(jnp.where(p0c == block + jj, 1.0, 0.0), axis=0, keepdims=True)
        via = dot(h1.astype(BF16), into1.astype(BF16))
        gsel[:, 0:block] = (via + h0 * (1.0 - any1)).astype(BF16)
        gsel[:, block : 2 * block] = (h1 * (1.0 - from0)).astype(BF16)
        own_ref[...] = jnp.broadcast_to((1.0 - any1) * (1.0 - any0), own_ref.shape)

    def panel_copy(p, other):
        return remote(pb.at[p], pb.at[p], pan_s.at[other], pan_r.at[p], (row, other))

    far = cols_n // 2

    def panel_far(action):
        for p in range(2):
            @pl.when(col == p)
            def _():
                action(panel_copy(p, far + p))

    def panel_near(action, first):
        for p in range(2):
            @pl.when(col == first + p)
            def _():
                for other in range(2, far, 2):
                    action(panel_copy(p, first + p + other))

    def core_copy(p):
        return remote(pb.at[p], pb.at[p], pan_s.at[0], pan_r.at[p], core_id)

    def panel_start():
        @pl.when(col == 0)
        def _():
            pb[0] = dot(o_ref[:, 0:block], up_ref[0]).astype(BF16)

        @pl.when(col == 1)
        def _():
            pb[1] = o_ref[:, 0:block]

        panel_far(lambda c: c.start())
        panel_near(lambda c: c.start(), 0)

    def panel_relay():
        for p in range(2):
            @pl.when(col == far + p)
            def _():
                panel_copy(p, far + p).wait_recv()

        panel_near(lambda c: c.start(), far)

    def panel_pass():
        for p in range(2):
            @pl.when(core == p)
            def _():
                @pl.when(lax.rem(col, far) != p)
                def _():
                    core_copy(p).wait_recv()

                core_copy(p).start()

    def panel_wait():
        for p in range(2):
            @pl.when(core != p)
            def _():
                core_copy(p).wait_recv()

    order = [k if i == 0 else zn - k for k in range(half, 0, -1) for i in range(2) if k < half or i == 0]

    def scatter_main(k):
        return remote(
            a_ref.at[pl.ds(k * per, per)], db.at[xl, k], sc_s.at[k], sc_r,
            (2 * k + xl, col),
        )

    def scatter_start(t):
        @pl.when(is_root)
        def _():
            for k in order[SC_N * t : SC_N * t + SC_N]:
                scatter_main(k).start()
            if t == 0:
                db[xl, 0] = a_ref[0:per, :]

    def scatter_wait():
        @pl.when(z != 0)
        def _():
            scatter_main(1).wait_recv()

    def t_piece(part, j, k):
        if j == 0:
            return te.at[part, k]
        return tb.at[:, j - 1, k] if j <= FULL else tb.at[part, j - 1, k]

    def d_piece(part, j, k):
        return db.at[part, k]

    t_stream = (t_piece, SUB + 1, T_HOP, tp_s, tp_r, tx_s, tx_r)
    d_stream = (d_piece, 1, D_HOP, dp_s, dp_r, dx_s, dx_r)

    def crosses(stream, j):
        if not D_CROSS and stream is d_stream:
            return False
        return stream is d_stream or j == 0 or j > FULL

    def along(stream, d, m, j, sender):
        piece, _, hop, ssem, rsem, _, _ = stream
        i = (m - 1) % hop + 1
        back = m - i if sender else m
        sign = 1 if d == 0 else -1
        ref = piece(xl, j, home(z - sign * back))
        slot = m if d == 0 else half + m
        return remote(ref, ref, ssem.at[slot, j], rsem.at[slot, j], at_z(sign * i))

    def across(stream, d, m, j):
        piece, _, _, _, _, ssem, rsem = stream
        ref = piece(xl, j, home(z - m if d == 0 else z + m))
        slot = m if d == 0 else half + m
        return remote(ref, ref, ssem.at[slot, j], rsem.at[slot, j], pair_id)

    def across_other(stream, d, m, j):
        piece, _, _, _, _, ssem, rsem = stream
        ref = piece(1 - xl, j, home(z - m if d == 0 else z + m))
        slot = m if d == 0 else half + m
        return remote(ref, ref, ssem.at[slot, j], rsem.at[slot, j], pair_id)

    last = (half, half - 1)

    def send_from(stream, d, u, j):
        hop = stream[2]
        for m in range(hop * u + 1, min(hop * u + hop, last[d]) + 1):
            along(stream, d, m, j, True).start()

    def gather_step(stream, u, js):
        hop = stream[2]
        for j in js:
            if u == 0:
                for d in range(2):
                    send_from(stream, d, 0, j)
                if crosses(stream, j):
                    across(stream, 0, 0, j).start()
        if u == 0:
            return
        for i in range(hop, 0, -1):
            m = hop * (u - 1) + i
            for j in js:
                for d in range(2):
                    if m <= last[d]:
                        along(stream, d, m, j, False).wait_recv()
                        if i == hop:
                            send_from(stream, d, u, j)
            for j in js:
                for d in range(2):
                    if m <= last[d] and crosses(stream, j):
                        across(stream, d, m, j).start()

    def steps(stream):
        return -(-half // stream[2]) + 1

    def slots():
        yield 0, 0
        for d in range(2):
            for m in range(1, last[d] + 1):
                yield d, m

    def cross_wait(stream):
        for j in range(stream[1]):
            for d, m in slots():
                if crosses(stream, j):
                    across_other(stream, d, m, j).wait_recv()

    def gather_sent(stream):
        for j in range(stream[1]):
            for d, m in slots():
                if crosses(stream, j):
                    across(stream, d, m, j).wait_send()
                if m:
                    along(stream, d, m, j, True).wait_send()

    def swap(s):
        if s < FULL:
            return remote(fin.at[s], xb.at[s], x_s.at[s], x_r.at[s], pair_id)
        return remote(fin.at[s, 1 - xl], xb.at[s, 0], x_s.at[s], x_r.at[s], pair_id)

    def swap_start():
        for s in range(SUB):
            plus(half - 1, s).wait_recv()
            minus(half - 2, s).wait_recv()
            fin[s] = cand[s, z] + rp[half - 1, s] + rm[half - 2, s]
            swap(s).start()

    def swap_wait(s):
        swap(s).wait_recv()
        if s < FULL:
            tb[:, s, z] = fin[s] + xb[s]
        else:
            tb[xl, s, z] = fin[s, xl] + xb[s, 0]

    def ext_copy(other):
        return remote(
            tb.at[xl, 0, z, :, pl.ds(0, block)], te.at[xl, z], e_s.at[other], e_r, (row, other)
        )

    def ext(action):
        for p in range(2):
            @pl.when(jnp.logical_and(col == p, source == p))
            def _():
                for other in range(cols_n):
                    if other != p:
                        action(ext_copy(other))

    def ext_start():
        ext(lambda c: c.start())

        @pl.when(col == source)
        def _():
            te[xl, z] = tb[xl, 0, z, :, 0:block]

    def ext_wait():
        @pl.when(col != source)
        def _():
            ext_copy(0).wait_recv()

    def cols(s):
        return slice(s * width, (s + 1) * width)

    def exchanged():
        own = own_ref[:, 0:1]
        g = gsel[...]
        for s in range(SUB):
            d0 = db[0, :, :, cols(s)].reshape(block, width)
            d1 = db[1, :, :, cols(s)].reshape(block, width)
            x = dot(g, jnp.concatenate([d0, d1], axis=0)) + own * a_ref[:, cols(s)].astype(F32)
            o_ref[:, cols(s)] = x.astype(BF16)

    d_next = [0]

    def d_step():
        if DO_D and d_next[0] < steps(d_stream):
            if d_next[0] == 0:
                scatter_wait()
            gather_step(d_stream, d_next[0], (0,))
            d_next[0] += 1

    reduce_step(0)
    if DO_D and SC_0 == 0:
        scatter_start(0)
    candidates()
    sources()
    for t in range(1, half):
        reduce_step(t)
        if DO_D and t >= SC_0:
            scatter_start(t - SC_0)
        if t >= D_START:
            d_step()
    swap_start()
    d_step()

    def panel_point(u):
        if DO_D and u == PAN_A:
            while d_next[0] < steps(d_stream):
                d_step()
            if D_CROSS:
                cross_wait(d_stream)
            exchanged()
            if DO_PAN:
                panel_start()
        if DO_PAN and DO_D and u == PAN_X:
            panel_relay()
        if DO_PAN and DO_D and u == PAN_B:
            panel_pass()

    panel_point(-1)
    swap_wait(0)
    ext_start()
    for s in range(1, SUB):
        swap_wait(s)
    main = tuple(range(1, SUB + 1))
    if DO_T:
        gather_step(t_stream, 0, main)
    panel_point(0)
    ext_wait()
    if DO_T:
        gather_step(t_stream, 0, (0,))
        for u in range(1, steps(t_stream)):
            gather_step(t_stream, u, main + (0,))
            panel_point(u)
        cross_wait(t_stream)
    if DO_D and DO_PAN:
        panel_wait()

    lo0, lo1, up0, up1 = lo_ref[0], lo_ref[1], up_ref[0], up_ref[1]

    if DO_COMP:
        ext0 = te[0].reshape(block, block)
        ext1 = te[1].reshape(block, block)
        lower_t = dot(ext1, up0).astype(BF16)

        def top(s):
            t0 = tb[0, s].reshape(block, width)
            t1 = tb[1, s].reshape(block, width)
            return t0, t1, dot(lo0, t0).astype(BF16)

        def second(t1, u0):
            t1u = (t1.astype(F32) - dot(lower_t, u0)).astype(BF16)
            return t1u, dot(lo1, t1u).astype(BF16)

        @pl.when(row == 0)
        def _():
            for s in range(SUB):
                o_ref[:, cols(s)] = top(s)[2]

            @pl.when(col == 0)
            def _():
                o_ref[:, 0:block] = tb[0, 0].reshape(block, width)[:, 0:block]

        @pl.when(row == 1)
        def _():
            for s in range(SUB):
                _, t1, u0 = top(s)
                t1u, u1 = second(t1, u0)
                o_ref[:, cols(s)] = u1
                if s == 0:
                    @pl.when(col == 1)
                    def _():
                        o_ref[:, 0:block] = t1u[:, 0:block]

            @pl.when(col == 0)
            def _():
                o_ref[:, 0:block] = lower_t

        @pl.when(row > 1)
        def _():
            l0 = pb[0]
            u0e = dot(lo0, ext0).astype(BF16)
            y1 = (pb[1].astype(F32) - dot(l0, u0e)).astype(BF16)
            l1 = dot(y1, up1).astype(BF16)
            ll = jnp.concatenate([l0, l1], axis=1)
            for s in range(SUB):
                _, t1, u0 = top(s)
                _, u1 = second(t1, u0)
                uu = jnp.concatenate([u0, u1], axis=0)
                o_ref[:, cols(s)] = (o_ref[:, cols(s)].astype(F32) - dot(ll, uu)).astype(BF16)

            @pl.when(col == 0)
            def _():
                o_ref[:, 0:block] = l0

            @pl.when(col == 1)
            def _():
                o_ref[:, 0:block] = l1
    else:
        o_ref[...] = jnp.zeros_like(o_ref)

    if DO_D and DO_PAN:
        panel_far(lambda c: c.wait_send())
        panel_near(lambda c: c.wait_send(), 0)
        panel_near(lambda c: c.wait_send(), far)
        core_copy(0).wait_send()
    if DO_D:

        @pl.when(is_root)
        def _():
            for k in order:
                scatter_main(k).wait_send()

        gather_sent(d_stream)
    for s in range(SUB):
        for t in range(half):
            plus(t, s).wait_send()
            if t < half - 1:
                minus(t, s).wait_send()
        swap(s).wait_send()
    ext(lambda c: c.wait_send())
    if DO_T:
        gather_sent(t_stream)


def body(matrix, pivots, lower_inverse, upper_inverse):
    local_rows, local_cols = matrix.shape
    block = lower_inverse.shape[1]
    rows_n = lax.axis_size("row")
    cols_n = lax.axis_size("col")
    zn = rows_n // 2
    half = zn // 2
    per = block // zn
    width = local_cols // SUB
    sem = pltpu.SemaphoreType.DMA
    vmem = pltpu.VMEM
    tn = SUB + 1
    return pl.pallas_call(
        functools.partial(kernel, rows_n, cols_n),
        out_shape=jax.ShapeDtypeStruct((local_rows, local_cols), BF16),
        in_specs=[pl.BlockSpec(memory_space=pltpu.VMEM)] * 4,
        out_specs=pl.BlockSpec(memory_space=pltpu.VMEM),
        scratch_shapes=[
            vmem((SUB, zn, 2, per, width), BF16),
            vmem((2, SUB, 2, per, width), BF16),
            vmem((zn, 2, per, block), BF16),
            vmem((half, SUB, 2, per, width), BF16),
            vmem((half - 1, SUB, 2, per, width), BF16),
            vmem((SUB, 2, per, width), BF16),
            vmem((SUB, 2, per, width), BF16),
            vmem((2, SUB, zn, per, width), BF16),
            vmem((2, zn, per, block), BF16),
            vmem((2, zn, per, local_cols), BF16),
            vmem((2, block, block), BF16),
            vmem((block, 2 * block), BF16),
            vmem((block, 128), F32),
            sem((half, SUB)), sem((half, SUB)),
            sem((half - 1, SUB)), sem((half - 1, SUB)),
            sem((SUB,)), sem((SUB,)),
            sem((cols_n,)), sem(()),
            sem((2 * half, tn)), sem((2 * half, tn)),
            sem((2 * half, tn)), sem((2 * half, tn)),
            sem((2 * half, 1)), sem((2 * half, 1)),
            sem((2 * half, 1)), sem((2 * half, 1)),
            sem((cols_n,)), sem((2,)),
            sem((zn,)), sem(()),
        ],
        compiler_params=pltpu.CompilerParams(
            collective_id=0, has_side_effects=True, vmem_limit_bytes=56 << 20
        ),
    )(matrix, pivots, lower_inverse, upper_inverse)


def solution(mesh):
    placed = (P("row", "col"), P(), P(), P())
    return jax.shard_map(
        body, mesh=mesh, in_specs=placed, out_specs=P("row", "col"), check_vma=False
    )
```

time: 1410 us -> 95.1 us (0.07)
  waiting for transfers between devices: 1370 us -> 0 us
  Pallas kernels: 0 us -> 91.3 us
    psum x6 -> x0, waiting for transfers between devices: 1370 us -> none  [the longest x4 835 us: spread(): return lax.psum(kept, axis)]
    pallas_call x0 -> x1, Pallas kernels: none -> 91.3 us  [body(): pl.pallas_call(functools.partial(kernel, rows_n, cols_n), out_shape=jax.S...]
  transfers between devices with their start and end apart: 6 -> 0, of which waited for: 6 -> 0; matrix products, arithmetic and copies ran while one was open for 0% -> 0% of each run, Pallas kernels for 0% -> 0%
where the time goes in v2:
time: 95.1 us; the launch traced here: 93.4 us
  Pallas kernels  91.3 us (96%)
  local copies, waits for them, and re-layouts  2.06 us (2%)
    pallas_call x1, Pallas kernels, body(): pl.pallas_call(functools.partial(kernel, rows_n, cols_n), out_shape=jax.S...  91.3 us
    unnamed x1, local copies, waits for them, and re-layouts  2.06 us

profile of v2, /device:TPU:24, one launch (start us, length us, event | category | flops | bytes accessed | tf_op | source)
XLA Modules:
  0.0 93.4 jit_solution(10294363289956913074)
XLA Ops:
  0.0 91.3 %shard_map.46 = bf16[256,1536]{1,0:T(8,128)(2,1)} custom-call(bf16[256,1536]{1,0:T(8,128)(2,1)} %a_ref.1, s32[2,256]{1,0:T(2,128)} %piv_ref.1, bf16[2,256,256]{2,1,0:T(8,128)(2,1)} %lo_ref.1, bf16[2,256,256]{2,1,0:T(8,128)(2,1)} %up_ref.1), custom_call_target="tpu_custom_call" | custom-call | tf_op jit(solution)/shard_map/pallas_call | solution.py:533
  91.4 2.1 %copy.6 = bf16[256,1536]{1,0:T(8,128)(2,1)} copy(bf16[256,1536]{1,0:T(8,128)(2,1)} %shard_map.46) | data formatting | bytes 1572864

commit v3 on v2

--- a/solution.py
+++ b/solution.py
@@ -10,21 +10,14 @@
 MESH = pl.DeviceIdType.MESH
 F32 = jnp.float32
 BF16 = jnp.bfloat16
-SUB = 3
+SUB = 2
 T_HOP = 2
 D_HOP = 2
-FULL = 0
 D_START = 2
+SC_N = 15
 PAN_A = 0
 PAN_X = 2
 PAN_B = 3
-DO_D = True
-DO_COMP = True
-DO_T = True
-DO_PAN = True
-D_CROSS = True
-SC_N = 15
-SC_0 = 0
 
 
 def dot(a, b):
@@ -34,7 +27,7 @@
 def kernel(
     rows_n, cols_n,
     a_ref, piv_ref, lo_ref, up_ref, o_ref,
-    cand, lead, selh, rp, rm, fin, xb, tb, te, db, pb, gsel, own_ref,
+    cand, lead, selh, rp, rm, xr, tb, te, db, pb, gsel, own_ref,
     rp_s, rp_r, rm_s, rm_r, x_s, x_r, e_s, e_r,
     tp_s, tp_r, tx_s, tx_r, dp_s, dp_r, dx_s, dx_r,
     pan_s, pan_r, sc_s, sc_r,
@@ -100,7 +93,7 @@
         sel = selh[firsts[d]].reshape(2 * per, block)
         for s in range(SUB):
             part = dot(sel, a_ref[:, s * width : (s + 1) * width]).astype(BF16)
-            lead[d, s] = part.reshape(2, per, width)
+            lead[d, :, s] = part.reshape(2, per, width)
 
     waits = 2 * reach + 2 + jnp.where(col < 2, cols_n - 1, 0) + jnp.where(col // 2 == cols_n // 4, cols_n // 4 - 1, 0) + jnp.where(is_root, zn - 1, 0)
     pl.semaphore_wait(barrier, waits)
@@ -111,33 +104,49 @@
             device_id=dest, device_id_type=MESH,
         )
 
+    def turn_home(i):
+        return home(z + half - i // 2) if i % 2 == 0 or i == zn - 1 else home(z - half + 1 + i // 2)
+
+    order_homes = [turn_home(i) for i in range(zn - 1)] + [z]
+
+    def give(i):
+        src = lead.at[i, 1 - xl] if i < 2 else cand.at[order_homes[i], 1 - xl]
+        return remote(src, xr.at[i], x_s.at[i], x_r.at[i], pair_id)
+
     def plus(t, s):
-        src = lead.at[0, s] if t == 0 else rp.at[t - 1, s]
+        src = lead.at[0, xl, s] if t == 0 else rp.at[t - 1, s]
         return remote(src, rp.at[t, s], rp_s.at[t, s], rp_r.at[t, s], at_z(1))
 
     def minus(t, s):
-        src = lead.at[1, s] if t == 0 else rm.at[t - 1, s]
+        src = lead.at[1, xl, s] if t == 0 else rm.at[t - 1, s]
         return remote(src, rm.at[t, s], rm_s.at[t, s], rm_r.at[t, s], at_z(-1))
 
     def reduce_step(t):
-        for s in range(SUB):
-            if t == 0:
-                plus(0, s).start()
-                minus(0, s).start()
-                continue
+        if t == 0:
+            for d, chain in ((0, plus), (1, minus)):
+                give(d).wait_recv()
+                lead[d, xl] = lead[d, xl] + xr[d]
+                for s in range(SUB):
+                    chain(0, s).start()
+            return
+        give(2 * t).wait_recv()
+        if t < half - 1:
+            give(2 * t + 1).wait_recv()
+        for s in range(SUB):
             plus(t - 1, s).wait_recv()
-            rp[t - 1, s] = rp[t - 1, s] + cand[s, home(z + half - t)]
+            rp[t - 1, s] = rp[t - 1, s] + (cand[order_homes[2 * t], xl, s] + xr[2 * t, s])
             plus(t, s).start()
             if t < half - 1:
+                i = 2 * t + 1
                 minus(t - 1, s).wait_recv()
-                rm[t - 1, s] = rm[t - 1, s] + cand[s, home(z - half + 1 + t)]
+                rm[t - 1, s] = rm[t - 1, s] + (cand[order_homes[i], xl, s] + xr[i, s])
                 minus(t, s).start()
 
     def candidates():
         for s in range(SUB):
             sel = selh[...].reshape(zn * 2 * per, block)
             part = dot(sel, a_ref[:, s * width : (s + 1) * width]).astype(BF16)
-            cand[s] = part.reshape(zn, 2, per, width)
+            cand[:, :, s] = part.reshape(zn, 2, per, width)
 
     def sources():
         h0 = jnp.where(base + ii == p0r, 1.0, 0.0)
@@ -230,20 +239,13 @@
             scatter_main(1).wait_recv()
 
     def t_piece(part, j, k):
-        if j == 0:
-            return te.at[part, k]
-        return tb.at[:, j - 1, k] if j <= FULL else tb.at[part, j - 1, k]
+        return te.at[part, k] if j == 0 else tb.at[part, j - 1, k]
 
     def d_piece(part, j, k):
         return db.at[part, k]
 
     t_stream = (t_piece, SUB + 1, T_HOP, tp_s, tp_r, tx_s, tx_r)
     d_stream = (d_piece, 1, D_HOP, dp_s, dp_r, dx_s, dx_r)
-
-    def crosses(stream, j):
-        if not D_CROSS and stream is d_stream:
-            return False
-        return stream is d_stream or j == 0 or j > FULL
 
     def along(stream, d, m, j, sender):
         piece, _, hop, ssem, rsem, _, _ = stream
@@ -279,8 +281,7 @@
             if u == 0:
                 for d in range(2):
                     send_from(stream, d, 0, j)
-                if crosses(stream, j):
-                    across(stream, 0, 0, j).start()
+                across(stream, 0, 0, j).start()
         if u == 0:
             return
         for i in range(hop, 0, -1):
@@ -293,7 +294,7 @@
                             send_from(stream, d, u, j)
             for j in js:
                 for d in range(2):
-                    if m <= last[d] and crosses(stream, j):
+                    if m <= last[d]:
                         across(stream, d, m, j).start()
 
     def steps(stream):
@@ -308,35 +309,21 @@
     def cross_wait(stream):
         for j in range(stream[1]):
             for d, m in slots():
-                if crosses(stream, j):
-                    across_other(stream, d, m, j).wait_recv()
+                across_other(stream, d, m, j).wait_recv()
 
     def gather_sent(stream):
         for j in range(stream[1]):
             for d, m in slots():
-                if crosses(stream, j):
-                    across(stream, d, m, j).wait_send()
+                across(stream, d, m, j).wait_send()
                 if m:
                     along(stream, d, m, j, True).wait_send()
 
-    def swap(s):
-        if s < FULL:
-            return remote(fin.at[s], xb.at[s], x_s.at[s], x_r.at[s], pair_id)
-        return remote(fin.at[s, 1 - xl], xb.at[s, 0], x_s.at[s], x_r.at[s], pair_id)
-
-    def swap_start():
-        for s in range(SUB):
-            plus(half - 1, s).wait_recv()
-            minus(half - 2, s).wait_recv()
-            fin[s] = cand[s, z] + rp[half - 1, s] + rm[half - 2, s]
-            swap(s).start()
-
-    def swap_wait(s):
-        swap(s).wait_recv()
-        if s < FULL:
-            tb[:, s, z] = fin[s] + xb[s]
-        else:
-            tb[xl, s, z] = fin[s, xl] + xb[s, 0]
+    def own_rows(s):
+        i = zn - 1
+        plus(half - 1, s).wait_recv()
+        minus(half - 2, s).wait_recv()
+        mine = cand[z, xl, s] + xr[i, s]
+        tb[xl, s, z] = mine + rp[half - 1, s] + rm[half - 2, s]
 
     def ext_copy(other):
         return remote(
@@ -378,144 +365,134 @@
     d_next = [0]
 
     def d_step():
-        if DO_D and d_next[0] < steps(d_stream):
+        if d_next[0] < steps(d_stream):
             if d_next[0] == 0:
                 scatter_wait()
             gather_step(d_stream, d_next[0], (0,))
             d_next[0] += 1
 
+    def panel_point(u):
+        if u == PAN_A:
+            while d_next[0] < steps(d_stream):
+                d_step()
+            cross_wait(d_stream)
+            exchanged()
+            panel_start()
+        if u == PAN_X:
+            panel_relay()
+        if u == PAN_B:
+            panel_pass()
+
+    give(0).start()
+    give(1).start()
+    scatter_start(0)
+    candidates()
+    for i in range(2, zn):
+        give(i).start()
     reduce_step(0)
-    if DO_D and SC_0 == 0:
-        scatter_start(0)
-    candidates()
     sources()
     for t in range(1, half):
         reduce_step(t)
-        if DO_D and t >= SC_0:
-            scatter_start(t - SC_0)
+        if SC_N < 15:
+            scatter_start(t)
         if t >= D_START:
             d_step()
-    swap_start()
-    d_step()
-
-    def panel_point(u):
-        if DO_D and u == PAN_A:
-            while d_next[0] < steps(d_stream):
-                d_step()
-            if D_CROSS:
-                cross_wait(d_stream)
-            exchanged()
-            if DO_PAN:
-                panel_start()
-        if DO_PAN and DO_D and u == PAN_X:
-            panel_relay()
-        if DO_PAN and DO_D and u == PAN_B:
-            panel_pass()
-
-    panel_point(-1)
-    swap_wait(0)
-    ext_start()
-    for s in range(1, SUB):
-        swap_wait(s)
+    give(zn - 1).wait_recv()
+    for s in range(SUB):
+        own_rows(s)
+        if s == 0:
+            ext_start()
     main = tuple(range(1, SUB + 1))
-    if DO_T:
-        gather_step(t_stream, 0, main)
+    gather_step(t_stream, 0, main)
     panel_point(0)
     ext_wait()
-    if DO_T:
-        gather_step(t_stream, 0, (0,))
-        for u in range(1, steps(t_stream)):
-            gather_step(t_stream, u, main + (0,))
-            panel_point(u)
-        cross_wait(t_stream)
-    if DO_D and DO_PAN:
-        panel_wait()
+    gather_step(t_stream, 0, (0,))
+    for u in range(1, steps(t_stream)):
+        gather_step(t_stream, u, main + (0,))
+        panel_point(u)
+    cross_wait(t_stream)
+    panel_wait()
 
     lo0, lo1, up0, up1 = lo_ref[0], lo_ref[1], up_ref[0], up_ref[1]
 
-    if DO_COMP:
-        ext0 = te[0].reshape(block, block)
-        ext1 = te[1].reshape(block, block)
-        lower_t = dot(ext1, up0).astype(BF16)
-
-        def top(s):
-            t0 = tb[0, s].reshape(block, width)
-            t1 = tb[1, s].reshape(block, width)
-            return t0, t1, dot(lo0, t0).astype(BF16)
-
-        def second(t1, u0):
-            t1u = (t1.astype(F32) - dot(lower_t, u0)).astype(BF16)
-            return t1u, dot(lo1, t1u).astype(BF16)
-
-        @pl.when(row == 0)
-        def _():
-            for s in range(SUB):
-                o_ref[:, cols(s)] = top(s)[2]
-
-            @pl.when(col == 0)
-            def _():
-                o_ref[:, 0:block] = tb[0, 0].reshape(block, width)[:, 0:block]
-
-        @pl.when(row == 1)
-        def _():
-            for s in range(SUB):
-                _, t1, u0 = top(s)
-                t1u, u1 = second(t1, u0)
-                o_ref[:, cols(s)] = u1
-                if s == 0:
-                    @pl.when(col == 1)
-                    def _():
-                        o_ref[:, 0:block] = t1u[:, 0:block]
-
-            @pl.when(col == 0)
-            def _():
-                o_ref[:, 0:block] = lower_t
-
-        @pl.when(row > 1)
-        def _():
-            l0 = pb[0]
-            u0e = dot(lo0, ext0).astype(BF16)
-            y1 = (pb[1].astype(F32) - dot(l0, u0e)).astype(BF16)
-            l1 = dot(y1, up1).astype(BF16)
-            ll = jnp.concatenate([l0, l1], axis=1)
-            for s in range(SUB):
-                _, t1, u0 = top(s)
-                _, u1 = second(t1, u0)
-                uu = jnp.concatenate([u0, u1], axis=0)
-                o_ref[:, cols(s)] = (o_ref[:, cols(s)].astype(F32) - dot(ll, uu)).astype(BF16)
-
-            @pl.when(col == 0)
-            def _():
-                o_ref[:, 0:block] = l0
-
-            @pl.when(col == 1)
-            def _():
-                o_ref[:, 0:block] = l1
-    else:
-        o_ref[...] = jnp.zeros_like(o_ref)
-
-    if DO_D and DO_PAN:
-        panel_far(lambda c: c.wait_send())
-        panel_near(lambda c: c.wait_send(), 0)
-        panel_near(lambda c: c.wait_send(), far)
-        core_copy(0).wait_send()
-    if DO_D:
-
-        @pl.when(is_root)
-        def _():
-            for k in order:
-                scatter_main(k).wait_send()
-
-        gather_sent(d_stream)
+    ext0 = te[0].reshape(block, block)
+    ext1 = te[1].reshape(block, block)
+    lower_t = dot(ext1, up0).astype(BF16)
+
+    def top(s):
+        t0 = tb[0, s].reshape(block, width)
+        t1 = tb[1, s].reshape(block, width)
+        return t0, t1, dot(lo0, t0).astype(BF16)
+
+    def second(t1, u0):
+        t1u = (t1.astype(F32) - dot(lower_t, u0)).astype(BF16)
+        return t1u, dot(lo1, t1u).astype(BF16)
+
+    @pl.when(row == 0)
+    def _():
+        for s in range(SUB):
+            o_ref[:, cols(s)] = top(s)[2]
+
+        @pl.when(col == 0)
+        def _():
+            o_ref[:, 0:block] = tb[0, 0].reshape(block, width)[:, 0:block]
+
+    @pl.when(row == 1)
+    def _():
+        for s in range(SUB):
+            _, t1, u0 = top(s)
+            t1u, u1 = second(t1, u0)
+            o_ref[:, cols(s)] = u1
+            if s == 0:
+                @pl.when(col == 1)
+                def _():
+                    o_ref[:, 0:block] = t1u[:, 0:block]
+
+        @pl.when(col == 0)
+        def _():
+            o_ref[:, 0:block] = lower_t
+
+    @pl.when(row > 1)
+    def _():
+        l0 = pb[0]
+        u0e = dot(lo0, ext0).astype(BF16)
+        y1 = (pb[1].astype(F32) - dot(l0, u0e)).astype(BF16)
+        l1 = dot(y1, up1).astype(BF16)
+        ll = jnp.concatenate([l0, l1], axis=1)
+        for s in range(SUB):
+            _, t1, u0 = top(s)
+            _, u1 = second(t1, u0)
+            uu = jnp.concatenate([u0, u1], axis=0)
+            o_ref[:, cols(s)] = (o_ref[:, cols(s)].astype(F32) - dot(ll, uu)).astype(BF16)
+
+        @pl.when(col == 0)
+        def _():
+            o_ref[:, 0:block] = l0
+
+        @pl.when(col == 1)
+        def _():
+            o_ref[:, 0:block] = l1
+
+    panel_far(lambda c: c.wait_send())
+    panel_near(lambda c: c.wait_send(), 0)
+    panel_near(lambda c: c.wait_send(), far)
+    core_copy(0).wait_send()
+
+    @pl.when(is_root)
+    def _():
+        for k in order:
+            scatter_main(k).wait_send()
+
+    gather_sent(d_stream)
+    for i in range(zn):
+        give(i).wait_send()
     for s in range(SUB):
         for t in range(half):
             plus(t, s).wait_send()
             if t < half - 1:
                 minus(t, s).wait_send()
-        swap(s).wait_send()
     ext(lambda c: c.wait_send())
-    if DO_T:
-        gather_sent(t_stream)
+    gather_sent(t_stream)
 
 
 def body(matrix, pivots, lower_inverse, upper_inverse):
@@ -536,13 +513,12 @@
         in_specs=[pl.BlockSpec(memory_space=pltpu.VMEM)] * 4,
         out_specs=pl.BlockSpec(memory_space=pltpu.VMEM),
         scratch_shapes=[
-            vmem((SUB, zn, 2, per, width), BF16),
-            vmem((2, SUB, 2, per, width), BF16),
+            vmem((zn, 2, SUB, per, width), BF16),
+            vmem((2, 2, SUB, per, width), BF16),
             vmem((zn, 2, per, block), BF16),
-            vmem((half, SUB, 2, per, width), BF16),
-            vmem((half - 1, SUB, 2, per, width), BF16),
-            vmem((SUB, 2, per, width), BF16),
-            vmem((SUB, 2, per, width), BF16),
+            vmem((half, SUB, per, width), BF16),
+            vmem((half - 1, SUB, per, width), BF16),
+            vmem((zn, SUB, per, width), BF16),
             vmem((2, SUB, zn, per, width), BF16),
             vmem((2, zn, per, block), BF16),
             vmem((2, zn, per, local_cols), BF16),
@@ -551,7 +527,7 @@
             vmem((block, 128), F32),
             sem((half, SUB)), sem((half, SUB)),
             sem((half - 1, SUB)), sem((half - 1, SUB)),
-            sem((SUB,)), sem((SUB,)),
+            sem((zn,)), sem((zn,)),
             sem((cols_n,)), sem(()),
             sem((2 * half, tn)), sem((2 * half, tn)),
             sem((2 * half, tn)), sem((2 * half, tn)),

time: 95.1 us -> 89.8 us (0.944)
  Pallas kernels: 91.3 us -> 86.4 us
    pallas_call x1, Pallas kernels: 91.3 us -> 86.4 us  [body(): pl.pallas_call(functools.partial(kernel, rows_n, cols_n), out_shape=jax.S...]
where the time goes in v3:
time: 89.8 us; the launch traced here: 88.5 us
  Pallas kernels  86.4 us (96%)
  local copies, waits for them, and re-layouts  2.06 us (2%)
    pallas_call x1, Pallas kernels, body(): pl.pallas_call(functools.partial(kernel, rows_n, cols_n), out_shape=jax.S...  86.4 us
    unnamed x1, local copies, waits for them, and re-layouts  2.06 us

profile of v3, /device:TPU:24, one launch (start us, length us, event | category | flops | bytes accessed | tf_op | source)
XLA Modules:
  0.0 88.5 jit_solution(12061187914915443390)
XLA Ops:
  0.0 86.4 %shard_map.46 = bf16[256,1536]{1,0:T(8,128)(2,1)} custom-call(bf16[256,1536]{1,0:T(8,128)(2,1)} %a_ref.1, s32[2,256]{1,0:T(2,128)} %piv_ref.1, bf16[2,256,256]{2,1,0:T(8,128)(2,1)} %lo_ref.1, bf16[2,256,256]{2,1,0:T(8,128)(2,1)} %up_ref.1), custom_call_target="tpu_custom_call" | custom-call | tf_op jit(solution)/shard_map/pallas_call | solution.py:510
  86.5 2.1 %copy.6 = bf16[256,1536]{1,0:T(8,128)(2,1)} copy(bf16[256,1536]{1,0:T(8,128)(2,1)} %shard_map.46) | data formatting | bytes 1572864

commit v4 on v3

--- a/solution.py
+++ b/solution.py
@@ -18,6 +18,8 @@
 PAN_A = 0
 PAN_X = 2
 PAN_B = 3
+VLIM = 24
+D_MORE = 0
 
 
 def dot(a, b):
@@ -26,13 +28,14 @@
 
 def kernel(
     rows_n, cols_n,
-    a_ref, piv_ref, lo_ref, up_ref, o_ref,
+    a_hbm, piv_hbm, lo_hbm, up_hbm, o_ref,
+    piv_ref, a_ref, lo_ref, up_ref, load_sem,
     cand, lead, selh, rp, rm, xr, tb, te, db, pb, gsel, own_ref,
     rp_s, rp_r, rm_s, rm_r, x_s, x_r, e_s, e_r,
     tp_s, tp_r, tx_s, tx_r, dp_s, dp_r, dx_s, dx_r,
     pan_s, pan_r, sc_s, sc_r,
 ):
-    block = lo_ref.shape[1]
+    block = lo_hbm.shape[1]
     zn = rows_n // 2
     half = zn // 2
     width = cand.shape[-1]
@@ -77,6 +80,14 @@
     def _():
         greet((xl, col))
 
+    loads = [
+        pltpu.make_async_copy(src, dst, load_sem.at[i])
+        for i, (src, dst) in enumerate(((piv_hbm, piv_ref), (a_hbm, a_ref), (lo_hbm, lo_ref), (up_hbm, up_ref)))
+    ]
+    for load in loads:
+        load.start()
+    loads[0].wait()
+
     base = (row * block).astype(F32)
     ii = lax.broadcasted_iota(jnp.int32, (block, block), 0).astype(F32)
     jj = lax.broadcasted_iota(jnp.int32, (block, block), 1).astype(F32)
@@ -88,6 +99,7 @@
     q1c = p1c + jnp.sum(jnp.where(p1c == p0r, jj - p1c, 0.0), axis=1, keepdims=True)
     selh[:, 0] = jnp.where(p0c == base + jj, 1.0, 0.0).astype(BF16).reshape(zn, per, block)
     selh[:, 1] = jnp.where(q1c == base + jj, 1.0, 0.0).astype(BF16).reshape(zn, per, block)
+    loads[1].wait()
     firsts = (home(z + half), home(z - half + 1))
     for d in range(2):
         sel = selh[firsts[d]].reshape(2 * per, block)
@@ -306,10 +318,9 @@
             for m in range(1, last[d] + 1):
                 yield d, m
 
-    def cross_wait(stream):
-        for j in range(stream[1]):
-            for d, m in slots():
-                across_other(stream, d, m, j).wait_recv()
+    def cross_wait(stream, j):
+        for d, m in slots():
+            across_other(stream, d, m, j).wait_recv()
 
     def gather_sent(stream):
         for j in range(stream[1]):
@@ -375,7 +386,7 @@
         if u == PAN_A:
             while d_next[0] < steps(d_stream):
                 d_step()
-            cross_wait(d_stream)
+            cross_wait(d_stream, 0)
             exchanged()
             panel_start()
         if u == PAN_X:
@@ -387,6 +398,8 @@
     give(1).start()
     scatter_start(0)
     candidates()
+    loads[2].wait()
+    loads[3].wait()
     for i in range(2, zn):
         give(i).start()
     reduce_step(0)
@@ -402,15 +415,21 @@
         own_rows(s)
         if s == 0:
             ext_start()
+    if D_MORE > 0:
+        d_step()
     main = tuple(range(1, SUB + 1))
     gather_step(t_stream, 0, main)
+    if D_MORE > 1:
+        d_step()
     panel_point(0)
     ext_wait()
     gather_step(t_stream, 0, (0,))
     for u in range(1, steps(t_stream)):
         gather_step(t_stream, u, main + (0,))
+        if D_MORE > 2:
+            d_step()
         panel_point(u)
-    cross_wait(t_stream)
+    cross_wait(t_stream, 0)
     panel_wait()
 
     lo0, lo1, up0, up1 = lo_ref[0], lo_ref[1], up_ref[0], up_ref[1]
@@ -420,6 +439,7 @@
     lower_t = dot(ext1, up0).astype(BF16)
 
     def top(s):
+        cross_wait(t_stream, s + 1)
         t0 = tb[0, s].reshape(block, width)
         t1 = tb[1, s].reshape(block, width)
         return t0, t1, dot(lo0, t0).astype(BF16)
@@ -493,6 +513,10 @@
                 minus(t, s).wait_send()
     ext(lambda c: c.wait_send())
     gather_sent(t_stream)
+
+
+def pin(x):
+    return pltpu.with_memory_space_constraint(x, pltpu.MemorySpace.HBM)
 
 
 def body(matrix, pivots, lower_inverse, upper_inverse):
@@ -510,9 +534,19 @@
     return pl.pallas_call(
         functools.partial(kernel, rows_n, cols_n),
         out_shape=jax.ShapeDtypeStruct((local_rows, local_cols), BF16),
-        in_specs=[pl.BlockSpec(memory_space=pltpu.VMEM)] * 4,
+        in_specs=[
+            pl.BlockSpec(memory_space=pltpu.MemorySpace.HBM),
+            pl.BlockSpec(memory_space=pltpu.MemorySpace.HBM),
+            pl.BlockSpec(memory_space=pltpu.MemorySpace.HBM),
+            pl.BlockSpec(memory_space=pltpu.MemorySpace.HBM),
+        ],
         out_specs=pl.BlockSpec(memory_space=pltpu.VMEM),
         scratch_shapes=[
+            vmem(pivots.shape, jnp.int32),
+            vmem((local_rows, local_cols), BF16),
+            vmem(lower_inverse.shape, BF16),
+            vmem(upper_inverse.shape, BF16),
+            sem((4,)),
             vmem((zn, 2, SUB, per, width), BF16),
             vmem((2, 2, SUB, per, width), BF16),
             vmem((zn, 2, per, block), BF16),
@@ -537,9 +571,9 @@
             sem((zn,)), sem(()),
         ],
         compiler_params=pltpu.CompilerParams(
-            collective_id=0, has_side_effects=True, vmem_limit_bytes=56 << 20
+            collective_id=0, has_side_effects=True, vmem_limit_bytes=VLIM << 20
         ),
-    )(matrix, pivots, lower_inverse, upper_inverse)
+    )(pin(matrix), pin(pivots), pin(lower_inverse), pin(upper_inverse))
 
 
 def solution(mesh):

time: 89.8 us -> 87.1 us (0.970)
  the two profiles are of different devices: /device:TPU:24 before, /device:TPU:64 now
where the time goes in v4:
time: 87.1 us; the launch traced here: 86.9 us
  Pallas kernels  86 us (99%)
  local copies, waits for them, and re-layouts  0.88 us (1%)
    pallas_call x1, Pallas kernels, body(): pl.pallas_call(functools.partial(kernel, rows_n, cols_n), out_shape=jax.S...  86 us

profile of v4, /device:TPU:64, one launch (start us, length us, event | category | flops | bytes accessed | tf_op | source)
XLA Modules:
  0.0 86.9 jit_solution(3714939238995444801)
XLA Ops:
  0.0 86.0 %shard_map.46 = bf16[256,1536]{1,0:T(8,128)(2,1)S(1)} custom-call(bf16[256,1536]{1,0:T(8,128)(2,1)} %a_hbm.1, s32[2,256]{1,0:T(2,128)} %piv_hbm.1, bf16[2,256,256]{2,1,0:T(8,128)(2,1)} %lo_hbm.1, bf16[2,256,256]{2,1,0:T(8,128)(2,1)} %up_hbm.1), custom_call_target="tpu_custom_call" | custom-call | tf_op jit(solution)/shard_map/pallas_call | solution.py:534
  86.0 0.9 %copy.6 = bf16[256,1536]{1,0:T(8,128)(2,1)} copy(bf16[256,1536]{1,0:T(8,128)(2,1)S(1)} %shard_map.46) | data formatting | bytes 1572864

commit v5 on v4

--- a/solution.py
+++ b/solution.py
@@ -16,8 +16,8 @@
 D_START = 2
 SC_N = 15
 PAN_A = 0
-PAN_X = 2
-PAN_B = 3
+PAN_X = 1
+PAN_B = 2
 VLIM = 24
 D_MORE = 0
 

time: 87.1 us -> 87 us (level)
  the two profiles are of different devices: /device:TPU:64 before, /device:TPU:24 now
where the time goes in v5:
time: 87 us; the launch traced here: 85.2 us
  Pallas kernels  84.3 us (97%)
  local copies, waits for them, and re-layouts  0.88 us (1%)
    pallas_call x1, Pallas kernels, body(): pl.pallas_call(functools.partial(kernel, rows_n, cols_n), out_shape=jax.S...  84.3 us

profile of v5, /device:TPU:24, one launch (start us, length us, event | category | flops | bytes accessed | tf_op | source)
XLA Modules:
  0.0 85.2 jit_solution(14394334699822334232)
XLA Ops:
  0.0 84.3 %shard_map.46 = bf16[256,1536]{1,0:T(8,128)(2,1)S(1)} custom-call(bf16[256,1536]{1,0:T(8,128)(2,1)} %a_hbm.1, s32[2,256]{1,0:T(2,128)} %piv_hbm.1, bf16[2,256,256]{2,1,0:T(8,128)(2,1)} %lo_hbm.1, bf16[2,256,256]{2,1,0:T(8,128)(2,1)} %up_hbm.1), custom_call_target="tpu_custom_call" | custom-call | tf_op jit(solution)/shard_map/pallas_call | solution.py:534
  84.3 0.9 %copy.6 = bf16[256,1536]{1,0:T(8,128)(2,1)} copy(bf16[256,1536]{1,0:T(8,128)(2,1)S(1)} %shard_map.46) | data formatting | bytes 1572864
